TPU v7x, 32 devices: a whole 2x2x4 slice. The times are simulated.
32 devices in a mesh: frame: 8 (over z, y), head: 2 (over x), batch: 2 (over core).
Axes of the slice: x: 2, y: 2, z: 4, core: 2. Of those that a mesh axis runs over, the one named last changes fastest.
Arguments:
- tokens: bfloat16 [8192, 1536], P(('batch', 'frame')), parts along dimension 0, may hold values from -6 to 6
- query_weight: bfloat16 [1536, 1536], P(None, 'head'), may hold values from -0.15625 to 0.15625
- key_weight: bfloat16 [1536, 1536], P(None, 'head'), may hold values from -0.15625 to 0.15625
- value_weight: bfloat16 [1536, 1536], P(None, 'head'), may hold values from -0.15625 to 0.15625
- out_weight: bfloat16 [1536, 1536], P('head'), may hold values from -0.625 to 0.625
- block_mask: int32 [16, 4, 13], P(('batch', 'frame')), parts along dimension 0, may hold values from 0 to 1, as said below
- frame_level: int32 [64], P(('batch', 'frame')), parts along dimension 0, may hold values from 0 to 15
- modulation: float32 [16, 2, 1536], replicated, may hold values from -1.2 to 13
Outputs:
- layer_out: bfloat16 [8192, 1536], P(('batch', 'frame'), 'head'), parts along dimension 0
There are 2 independent parts, one for each index of `batch`. A program takes and returns all parts, laid end to end along the dimension named above; an argument that names none is the same for every part. Nothing has to cross between parts.
Inputs may be any that keep to these rules, and one draw needn't show every extreme that they name: `block_mask`: in span c every tile with key block below 1, and the tile of query block i with key block (1152) / 128 + i, is always 1; the share of the other tiles that are 1 differs from span to span.
All inputs are finite; a program needn't handle non-finite values.
Results may differ from a plain program's by a relative error of at most 0.01.
The roundings to bfloat16 on the way count: a program that leaves them out, or rounds other values in their place, can miss the bound.
Values may be sent and summed in bfloat16 or wider, within the bound.
A program may use at most 128 MiB of HBM per device.

v0:
```python
import math
import jax
import jax.numpy as jnp
from jax import lax
from jax.sharding import PartitionSpec as P

HEAD_DIM = 128
FRAME_TOK = 128
SINK = 128
TILE = 128


def broadcast(array, axis, root):
    mine = lax.axis_index(axis) == root
    return lax.psum(jnp.where(mine, array, jnp.zeros_like(array)), axis)


def from_behind(array, axis, by):
    length = lax.axis_size(axis)
    pairs = [(i, i + by) for i in range(length) if 0 <= i + by < length]
    return lax.ppermute(array, axis, pairs)


def visible(span_index, span_len, total_keys):
    key_place = jnp.arange(total_keys, dtype=jnp.int32)
    near_start = SINK + span_len
    own_start = SINK + 2 * span_len
    return (
        (key_place < SINK)
        | (key_place >= own_start)
        | (key_place >= near_start) & (span_index >= 1)
        | (key_place < near_start) & (span_index >= 2)
    )


def shards(
    tokens, query_weight, key_weight, value_weight, out_weight, block_mask, frame_level, modulation
):
    span_len, model_width = tokens.shape
    level_count = modulation.shape[0]
    frame_count = frame_level.shape[0]
    xfloat = tokens.astype(jnp.float32)
    mean_square = jnp.mean(xfloat * xfloat, axis=-1, keepdims=True)
    normed = xfloat * lax.rsqrt(mean_square + 1e-06)
    level_onehot = (
        frame_level[:, None] == jnp.arange(level_count, dtype=jnp.int32)[None, :]
    ).astype(jnp.float32)
    chosen = jnp.dot(
        level_onehot,
        modulation.reshape(level_count, 2 * model_width),
        precision=lax.Precision.HIGHEST,
    )
    chosen = chosen.reshape(frame_count, 1, 2, model_width)
    shaped = normed.reshape(frame_count, FRAME_TOK, model_width)
    modulated = (
        (shaped * (1.0 + chosen[:, :, 0]) + chosen[:, :, 1])
        .reshape(span_len, model_width)
        .astype(jnp.bfloat16)
    )
    score_scale = 1.0 / math.sqrt(HEAD_DIM)
    query_rows = (
        jnp.dot(modulated, query_weight, preferred_element_type=jnp.float32) * score_scale
    ).astype(jnp.bfloat16)
    key_value = jnp.stack(
        [
            jnp.dot(modulated, key_weight, preferred_element_type=jnp.float32).astype(jnp.bfloat16),
            jnp.dot(modulated, value_weight, preferred_element_type=jnp.float32).astype(
                jnp.bfloat16
            ),
        ]
    )
    sink_pair = broadcast(key_value[:, :SINK], "frame", 0)
    previous_pair = from_behind(key_value, "frame", 1)
    earlier_pair = from_behind(key_value, "frame", 2)
    window_pair = jnp.concatenate([sink_pair, earlier_pair, previous_pair, key_value], axis=1)
    local_width = query_weight.shape[1]
    local_heads = local_width // HEAD_DIM
    total_keys = window_pair.shape[1]
    key_rows = window_pair[0].reshape(total_keys, local_heads, HEAD_DIM)
    value_rows = window_pair[1].reshape(total_keys, local_heads, HEAD_DIM)
    queries = query_rows.reshape(span_len, local_heads, HEAD_DIM)
    tile_mask = block_mask[0]
    query_blocks, key_blocks = tile_mask.shape
    tile_full = jnp.broadcast_to(
        tile_mask[:, None, :, None], (query_blocks, TILE, key_blocks, TILE)
    ).reshape(span_len, total_keys)
    span_index = lax.axis_index("frame")
    allowed = (tile_full > 0) & visible(span_index, span_len, total_keys)[None, :]
    score_rows = jnp.einsum("qhd,khd->hqk", queries, key_rows, preferred_element_type=jnp.float32)
    masked_scores = jnp.where(allowed[None], score_rows, -1e30)
    row_peak = jnp.max(masked_scores, axis=-1, keepdims=True)
    softmax_num = jnp.where(allowed[None], jnp.exp(masked_scores - row_peak), 0.0)
    row_total = jnp.sum(softmax_num, axis=-1)
    weights_bf = softmax_num.astype(jnp.bfloat16)
    mixed_rows = jnp.einsum(
        "hqk,khd->qhd", weights_bf, value_rows, preferred_element_type=jnp.float32
    )
    attention_out = (
        (mixed_rows / row_total.T[:, :, None]).astype(jnp.bfloat16).reshape(span_len, local_width)
    )
    share_cols = model_width // lax.axis_size("head")
    col_start = lax.axis_index("head") * share_cols
    partial_rows = jnp.dot(attention_out, out_weight, preferred_element_type=jnp.float32)
    summed_rows = lax.psum_scatter(partial_rows, "head", scatter_dimension=1, tiled=True)
    residual_cols = lax.dynamic_slice_in_dim(xfloat, col_start, share_cols, 1)
    return (residual_cols + summed_rows).astype(jnp.bfloat16)


def solution(mesh):
    placed = (
        P(("batch", "frame"), None),
        P(None, "head"),
        P(None, "head"),
        P(None, "head"),
        P("head", None),
        P(("batch", "frame"), None, None),
        P(("batch", "frame")),
        P(),
    )
    return jax.shard_map(
        shards, mesh=mesh, in_specs=placed, out_specs=P(("batch", "frame"), "head"), check_vma=False
    )
```

profile of v0, /device:TPU:0, one launch (start us, length us, event | category | flops | bytes accessed | tf_op | source)
XLA Modules:
  0.0 194.5 jit_solution(17219739829432038658)
XLA Ops:
  6.5 0.0 copy-start
  6.5 0.0 all-reduce.2.cloned.1.call-start
  6.5 0.0 copy-start.1
  6.5 0.0 copy-start.6
  6.5 1.3 convolution_bitcast_fusion
  7.9 1.9 multiply_reduce_fusion
  9.8 0.0 copy-done.1
  9.8 0.5 fusion.8
  10.3 0.0 copy-done.6
  10.3 0.0 copy-start.3
  10.3 0.0 copy-start.7
  10.4 1.4 fusion.15
  11.7 0.0 copy-done.3
  11.8 0.8 copy-done.7
  12.6 1.4 fusion.14
  14.0 0.0 copy-start.2
  14.0 0.9 copy-done.2
  14.8 0.0 copy-start.5
  14.8 1.3 pad_maximum_fusion
  16.2 6.0 %collective-permute-start.1 = (bf16[2,512,768]{2,1,0:T(8,128)(2,1)}, bf16[2,512,768]{2,1,0:T(8,128)(2,1)}, u32[]{:S(2)}, u32[]{:S(2)}) collective-permute-start(bf16[2,512,768]{2,1,0:T(8,128)(2,1)} %pad_maximum_fusion), channel_id=1, source_target_pairs={{0,4},{4,8},{8,12},{12,16},{16,20},{20,24},{24,28},{1,5},{5,9},{9,... | collective-permute-start | bytes 4718600 | tf_op jit(solution)/shard_map/ppermute | solution.py:21
  22.2 3.5 %collective-permute-start = (bf16[2,512,768]{2,1,0:T(8,128)(2,1)}, bf16[2,512,768]{2,1,0:T(8,128)(2,1)}, u32[]{:S(2)}, u32[]{:S(2)}) collective-permute-start(bf16[2,512,768]{2,1,0:T(8,128)(2,1)} %pad_maximum_fusion), channel_id=1, source_target_pairs={{0,8},{4,12},{8,16},{12,20},{16,24},{20,28},{1,9},{5,13},{9,17},{1... | collective-permute-start | bytes 4718600 | tf_op jit(solution)/shard_map/ppermute | solution.py:21
  25.7 1.8 fusion.17
  27.4 0.0 all-reduce.2.cloned.1.call-update
  27.5 0.0 reduce-scatter.2.cloned.1.call-start
  27.5 0.0 copy-done.5
  27.5 0.1 copy.14
  27.7 0.5 broadcast_in_dim.35
  28.2 2.2 %bitcast_and_fusion = pred[512,1664]{0,1:T(8,128)(4,1)} fusion(pred[208,8,4,128]{3,2,1,0:T(4,128)(4,1)S(1)} %bitcast.63, pred[1664]{0:T(1024)(128)(4,1)S(1)} %fusion.23), kind=kLoop, calls=%fused_computation.9 | loop fusion | flops 851968 | bytes 1705600 | tf_op jit(solution)/shard_map/and | solution.py:88
  30.4 3.6 %copy.15 = pred[512,1664]{1,0:T(8,128)(4,1)} copy(pred[512,1664]{0,1:T(8,128)(4,1)} %bitcast_and_fusion) | data formatting | bytes 1703936 | tf_op jit(solution)/shard_map/and | solution.py:88
  34.0 4.4 %multiply_convert_fusion = bf16[512,768]{1,0:T(8,128)(2,1)} fusion(bf16[512,1536]{1,0:T(8,128)(2,1)} %copy-done.3, bf16[1536,768]{1,0:T(8,128)(2,1)} %param.9), kind=kOutput, calls=%fused_computation.22 | convolution fusion | flops 1208745984 | bytes 4718592 | tf_op jit(solution)/shard_map/dot_general | solution.py:62
  38.4 2.3 %copy.16 = bf16[512,768]{0,1:T(8,128)(2,1)} copy(bf16[512,768]{1,0:T(8,128)(2,1)} %multiply_convert_fusion) | data formatting | bytes 1572864 | tf_op jit(solution)/shard_map/convert_element_type | solution.py:63
  40.7 62.1 %all-reduce.2.cloned.1.call-done = bf16[2,128,768]{2,1,0:T(8,128)(2,1)} async-done(((bf16[2,128,768]{2,1,0:T(8,128)(2,1)}), bf16[2,128,768]{2,1,0:T(8,128)(2,1)}) %all-reduce.2.cloned.1.call-update) | async-done | bytes 393232 | tf_op jit(solution)/shard_map/psum | solution.py:15
  102.8 0.0 collective-permute-done.1
  102.8 0.0 collective-permute-done
  102.8 3.0 %maximum_maximum_fusion = bf16[2,1664,768]{2,1,0:T(8,128)(2,1)S(1)} fusion(bf16[1,512,768]{2,1,0:T(8,128)(2,1)S(1)} %fusion.15, bf16[1,512,768]{2,1,0:T(8,128)(2,1)} %copy-done.2, bf16[2,512,768]{2,1,0:T(8,128)(2,1)} %collective-permute-done.1, bf16[2,512,768]{2,1,0:T(8,128)(2,1)} %collective-permute-done, bf16[2,128,768]{2,1,0:T(8,128)(2,1)} %all-reduce.2.cloned.1.call-done), kind=kLoop, calls=%fused_computation.8 | loop fusion | flops 25559040 | bytes 10223616 | tf_op jit(solution)/shard_map/concatenate | solution.py:75
  105.8 2.6 %fusion.30 = (bf16[1,1664,768]{2,1,0:T(8,128)(2,1)}, bf16[1,1664,768]{2,1,0:T(8,128)(2,1)}) fusion(bf16[2,1664,768]{2,1,0:T(8,128)(2,1)S(1)} %maximum_maximum_fusion), kind=kLoop, calls=%fused_computation.49 | loop fusion | bytes 10223616 | tf_op jit(solution)/shard_map/slice | solution.py:79
  108.4 4.5 %copy.13 = bf16[1,1664,768]{1,2,0:T(8,128)(2,1)} copy(bf16[1,1664,768]{2,1,0:T(8,128)(2,1)} %get-tuple-element.6) | data formatting | bytes 5111808 | tf_op jit(solution)/shard_map/slice | solution.py:80
  113.0 0.0 copy-start.4
  113.0 4.6 %copy.17 = bf16[1,1664,768]{1,2,0:T(8,128)(2,1)} copy(bf16[1,1664,768]{2,1,0:T(8,128)(2,1)} %get-tuple-element.5) | data formatting | bytes 5111808 | tf_op jit(solution)/shard_map/slice | solution.py:79
  117.6 0.0 copy-done.4
  117.6 13.3 %fusion.31 = (f32[6,512]{1,0:T(8,128)S(1)}, bf16[6,512,1664]{2,1,0:T(8,128)(2,1)}) fusion(pred[512,1664]{1,0:T(8,128)(4,1)S(1)} %copy-done.4, bf16[512,6,128]{0,2,1:T(8,128)(2,1)} %bitcast.67, bf16[1664,6,128]{0,2,1:T(8,128)(2,1)} %bitcast.65), kind=kOutput, calls=%fused_computation.50 | convolution fusion | flops 1334183552 | bytes 14430208 | tf_op jit(solution)/shard_map/sub | solution.py:92
  130.9 8.1 %fusion.11 = bf16[512,6,128]{0,2,1:T(8,128)(2,1)S(1)} fusion(bf16[1664,6,128]{0,2,1:T(8,128)(2,1)} %bitcast.64, bf16[6,512,1664]{2,1,0:T(8,128)(2,1)} %get-tuple-element.10, f32[512,6]{0,1:T(8,128)S(1)} %bitcast.69), kind=kOutput, calls=%fused_computation.20 | convolution fusion | flops 1309409280 | bytes 13578240 | tf_op jit(solution)/shard_map/hqk,khd->qhd/dot_general | solution.py:95
  138.9 0.0 copy-done
  139.0 3.1 %fusion.32 = f32[512,1536]{1,0:T(8,128)} fusion(bf16[512,768]{0,1:T(8,128)(2,1)S(1)} %bitcast.66, bf16[768,1536]{1,0:T(8,128)(2,1)S(1)} %copy-done), kind=kOutput, calls=%fused_computation.52 | convolution fusion | flops 1207959552 | bytes 6291456 | tf_op jit(solution)/shard_map/dot_general | solution.py:103
  142.0 0.0 reduce-scatter.2.cloned.1.call-update
  142.1 3.5 %convert_element_type.25 = f32[512,1536]{1,0:T(8,128)} convert(bf16[512,1536]{1,0:T(8,128)(2,1)} %param.8) | non-fusion elementwise | flops 786432 | bytes 4718592 | tf_op jit(solution)/shard_map/convert_element_type | solution.py:42
  145.6 39.2 %reduce-scatter.2.cloned.1.call-done = f32[512,768]{1,0:T(8,128)} async-done(((f32[512,1536]{1,0:T(8,128)}), f32[512,768]{1,0:T(8,128)}) %reduce-scatter.2.cloned.1.call-update) | async-done | bytes 1572880 | tf_op jit(solution)/shard_map/reduce_scatter | solution.py:104
  184.7 2.9 %add_convert_fusion = bf16[512,768]{1,0:T(8,128)(2,1)} fusion(f32[512,768]{1,0:T(8,128)} %reduce-scatter.2.cloned.1.call-done, f32[512,1536]{1,0:T(8,128)} %convert_element_type.25, s32[]{:T(128)S(6)} %select_n.18), kind=kLoop, calls=%fused_computation.21 | loop fusion | flops 786432 | bytes 3932164 | tf_op jit(solution)/shard_map/convert_element_type | solution.py:106
  (4 shorter events, 0.0 us)
Async XLA Ops:
  6.5 132.4 %copy-start = (bf16[768,1536]{1,0:T(8,128)(2,1)S(1)}, bf16[768,1536]{1,0:T(8,128)(2,1)}, u32[]{:S(2)}) copy-start(bf16[768,1536]{1,0:T(8,128)(2,1)} %param.12) | copy-start | bytes 7077892
  6.5 96.3 %all-reduce.2.cloned.1.call-start = ((), (), s32[]{:S(2)}) async-start(), calls=%async_computation.1 | async-start | bytes 786432 | tf_op jit(solution)/shard_map/psum | solution.py:15
  6.5 3.2 %copy-start.1 = (bf16[512,1536]{1,0:T(8,128)(2,1)S(1)}, bf16[512,1536]{1,0:T(8,128)(2,1)}, u32[]{:S(2)}) copy-start(bf16[512,1536]{1,0:T(8,128)(2,1)} %param.8) | copy-start | bytes 4718596
  6.5 3.8 %copy-start.6 = (bf16[1536,768]{1,0:T(8,128)(2,1)S(1)}, bf16[1536,768]{1,0:T(8,128)(2,1)}, u32[]{:S(2)}) copy-start(bf16[1536,768]{1,0:T(8,128)(2,1)} %param.11) | copy-start | bytes 7077892
  10.3 1.4 copy-start.3
  10.3 2.2 %copy-start.7 = (bf16[1536,768]{1,0:T(8,128)(2,1)S(1)}, bf16[1536,768]{1,0:T(8,128)(2,1)}, u32[]{:S(2)}) copy-start(bf16[1536,768]{1,0:T(8,128)(2,1)} %param.10) | copy-start | bytes 7077892
  14.0 0.9 copy-start.2
  14.8 12.7 %copy-start.5 = (s32[1,4,13]{2,1,0:T(4,128)S(1)}, s32[1,4,13]{2,1,0:T(4,128)}, u32[]{:S(2)}) copy-start(s32[1,4,13]{2,1,0:T(4,128)} %param.13) | copy-start | bytes 628
  16.2 86.7 %collective-permute-start.1 = (bf16[2,512,768]{2,1,0:T(8,128)(2,1)}, bf16[2,512,768]{2,1,0:T(8,128)(2,1)}, u32[]{:S(2)}, u32[]{:S(2)}) collective-permute-start(bf16[2,512,768]{2,1,0:T(8,128)(2,1)} %pad_maximum_fusion), channel_id=1, source_target_pairs={{0,4},{4,8},{8,12},{12,16},{16,20},{20,24},{24,28},{1,5},{5,9},{9,... | collective-permute-start | bytes 4718600 | tf_op jit(solution)/shard_map/ppermute | solution.py:21
  22.2 80.7 %collective-permute-start = (bf16[2,512,768]{2,1,0:T(8,128)(2,1)}, bf16[2,512,768]{2,1,0:T(8,128)(2,1)}, u32[]{:S(2)}, u32[]{:S(2)}) collective-permute-start(bf16[2,512,768]{2,1,0:T(8,128)(2,1)} %pad_maximum_fusion), channel_id=1, source_target_pairs={{0,8},{4,12},{8,16},{12,20},{16,24},{20,28},{1,9},{5,13},{9,17},{1... | collective-permute-start | bytes 4718600 | tf_op jit(solution)/shard_map/ppermute | solution.py:21
  27.5 157.2 %reduce-scatter.2.cloned.1.call-start = ((), (), s32[]{:S(2)}) async-start(), calls=%async_computation.2 | async-start | bytes 4718592 | tf_op jit(solution)/shard_map/reduce_scatter | solution.py:104
  113.0 4.6 %copy-start.4 = (pred[512,1664]{1,0:T(8,128)(4,1)S(1)}, pred[512,1664]{1,0:T(8,128)(4,1)}, u32[]{:S(2)}) copy-start(pred[512,1664]{1,0:T(8,128)(4,1)} %copy.15) | copy-start | bytes 2555908
Sparse Core Ops, SparseCore 0:
  27.6 75.2 all-reduce.1
  142.2 42.4 reduce-scatter.1
where the time goes:
time: 195 us; the launch traced here: 194 us
  waiting for transfers between devices  101 us (52%)
  matrix products  32.9 us (17%)
  local copies, waits for them, and re-layouts  20 us (10%)
  other arithmetic  17.1 us (9%)
  between operations  13.5 us (7%)
  starting transfers between devices  9.55 us (5%)
    psum x1, waiting for transfers between devices, broadcast(): return lax.psum(jnp.where(mine, array, jnp.zeros_like(array)), axis)  62.1 us
    reduce_scatter x1, waiting for transfers between devices, shards(): lax.psum_scatter(partial_rows, 'head', scatter_dimension=1, tiled=True)  39.2 us
    sub x1, matrix products, shards(): masked_scores - row_peak  13.3 us
    ppermute x2, starting transfers between devices, from_behind(): return lax.ppermute(array, axis, pairs)  9.51 us
    dot_general x1, matrix products, shards(): jnp.einsum('hqk,khd->qhd', weights_bf, value_rows, preferred_element_type...  8.06 us
    slice x2, local copies, waits for them, and re-layouts, shards(): key_rows = window_pair[0].reshape(total_keys, local_heads, HEAD_DIM)  7.2 us
    slice x1, local copies, waits for them, and re-layouts, shards(): value_rows = window_pair[1].reshape(total_keys, local_heads, HEAD_DIM)  4.53 us
    dot_general x1, matrix products, shards(): jnp.dot(modulated, query_weight, preferred_element_type=jnp.float32)  4.41 us
  transfers between devices with their start and end apart: 4, of which 2 were waited for; matrix products, arithmetic and copies ran while one was open for 9% of the time, Pallas kernels for 0%

commit v1 on v0

--- a/solution.py
+++ b/solution.py
@@ -12,7 +12,7 @@
 
 def broadcast(array, axis, root):
     mine = lax.axis_index(axis) == root
-    return lax.psum(jnp.where(mine, array, jnp.zeros_like(array)), axis)
+    return jnp.sum(lax.all_gather(jnp.where(mine, array, jnp.zeros_like(array)), axis), axis=0)
 
 
 def from_behind(array, axis, by):

time: 195 us -> 225 us (1.15)
  waiting for transfers between devices: 101 us -> 128 us
  other arithmetic: 17.1 us -> 20.5 us
    psum x1 -> x0, waiting for transfers between devices: 62.1 us -> none  [broadcast(): return lax.psum(jnp.where(mine, array, jnp.zeros_like(array)), axis)]
    all_gather x0 -> x1, waiting for transfers between devices: none -> 59.5 us  [broadcast(): lax.all_gather(jnp.where(mine, array, jnp.zeros_like(array)), axis)]
    reduce_scatter x1, waiting for transfers between devices: 39.2 us -> 68.2 us  [shards(): lax.psum_scatter(partial_rows, 'head', scatter_dimension=1, tiled=True)]
    reduce_sum x0 -> x1, other arithmetic: none -> 2.44 us  [broadcast(): jnp.sum(lax.all_gather(jnp.where(mine, array, jnp.zeros_like(array)), axi...]
  transfers between devices with their start and end apart: 4 -> 4, of which waited for: 2 -> 2; matrix products, arithmetic and copies ran while one was open for 9% -> 10% of each run, Pallas kernels for 0% -> 0%
where the time goes in v1:
time: 225 us; the launch traced here: 224 us
  waiting for transfers between devices  128 us (57%)
  matrix products  33.8 us (15%)
  other arithmetic  20.5 us (9%)
  local copies, waits for them, and re-layouts  19.1 us (8%)
  between operations  13.5 us (6%)
  starting transfers between devices  9.55 us (4%)
    reduce_scatter x1, waiting for transfers between devices, shards(): lax.psum_scatter(partial_rows, 'head', scatter_dimension=1, tiled=True)  68.2 us
    all_gather x1, waiting for transfers between devices, broadcast(): lax.all_gather(jnp.where(mine, array, jnp.zeros_like(array)), axis)  59.5 us
    sub x1, matrix products, shards(): masked_scores - row_peak  13.3 us
    ppermute x2, starting transfers between devices, from_behind(): return lax.ppermute(array, axis, pairs)  9.51 us
    dot_general x1, matrix products, shards(): jnp.einsum('hqk,khd->qhd', weights_bf, value_rows, preferred_element_type...  8.06 us
    slice x2, local copies, waits for them, and re-layouts, shards(): key_rows = window_pair[0].reshape(total_keys, local_heads, HEAD_DIM)  7.26 us
  transfers between devices with their start and end apart: 4, of which 2 were waited for; matrix products, arithmetic and copies ran while one was open for 10% of the time, Pallas kernels for 0%

profile of v1, /device:TPU:0, one launch (start us, length us, event | category | flops | bytes accessed | tf_op | source)
XLA Modules:
  0.0 224.2 jit_solution(11528052181245229688)
XLA Ops:
  6.5 0.0 copy-start
  6.5 0.0 all-gather.3.cloned.1.call-start
  6.5 0.0 copy-start.1
  6.5 0.0 copy-start.5
  6.5 1.3 convolution_bitcast_fusion
  7.9 1.9 multiply_reduce_fusion
  9.8 0.0 copy-done.1
  9.8 0.5 fusion.8
  10.3 0.0 copy-done.5
  10.3 0.0 copy-start.2
  10.3 0.0 copy-start.6
  10.4 1.4 fusion.15
  11.7 0.0 copy-done.2
  11.8 0.8 copy-done.6
  12.6 2.3 %fusion.14 = bf16[1,512,768]{2,1,0:T(8,128)(2,1)} fusion(bf16[512,1536]{1,0:T(8,128)(2,1)S(1)} %fusion.8, bf16[1536,768]{1,0:T(8,128)(2,1)S(1)} %copy-done.6), kind=kOutput, calls=%fused_computation.25 | convolution fusion | flops 1208352768 | bytes 4718592 | tf_op jit(solution)/shard_map/dot_general | solution.py:66
  14.8 0.0 copy-start.4
  14.8 1.8 fusion.17
  16.6 0.0 all-gather.3.cloned.1.call-update
  16.6 0.0 reduce-scatter.2.cloned.1.call-start
  16.7 2.4 %pad_maximum_fusion = bf16[2,512,768]{2,1,0:T(8,128)(2,1)} fusion(bf16[1,512,768]{2,1,0:T(8,128)(2,1)S(1)} %fusion.15, bf16[1,512,768]{2,1,0:T(8,128)(2,1)} %fusion.14), kind=kLoop, calls=%fused_computation.17 | loop fusion | flops 786432 | bytes 3145728 | tf_op jit(solution)/shard_map/stack | solution.py:64
  19.1 6.0 %collective-permute-start.1 = (bf16[2,512,768]{2,1,0:T(8,128)(2,1)}, bf16[2,512,768]{2,1,0:T(8,128)(2,1)}, u32[]{:S(2)}, u32[]{:S(2)}) collective-permute-start(bf16[2,512,768]{2,1,0:T(8,128)(2,1)} %pad_maximum_fusion), channel_id=1, source_target_pairs={{0,4},{4,8},{8,12},{12,16},{16,20},{20,24},{24,28},{1,5},{5,9},{9,... | collective-permute-start | bytes 4718600 | tf_op jit(solution)/shard_map/ppermute | solution.py:21
  25.1 3.5 %collective-permute-start = (bf16[2,512,768]{2,1,0:T(8,128)(2,1)}, bf16[2,512,768]{2,1,0:T(8,128)(2,1)}, u32[]{:S(2)}, u32[]{:S(2)}) collective-permute-start(bf16[2,512,768]{2,1,0:T(8,128)(2,1)} %pad_maximum_fusion), channel_id=1, source_target_pairs={{0,8},{4,12},{8,16},{12,20},{16,24},{20,28},{1,9},{5,13},{9,17},{1... | collective-permute-start | bytes 4718600 | tf_op jit(solution)/shard_map/ppermute | solution.py:21
  28.6 0.0 copy-done.4
  28.6 0.1 copy.22
  28.7 0.5 broadcast_in_dim.35
  29.3 2.0 bitcast_and_fusion
  31.3 3.5 %copy.23 = pred[512,1664]{1,0:T(8,128)(4,1)} copy(pred[512,1664]{0,1:T(8,128)(4,1)} %bitcast_and_fusion) | data formatting | bytes 1703936 | tf_op jit(solution)/shard_map/and | solution.py:88
  34.8 4.4 %multiply_convert_fusion = bf16[512,768]{1,0:T(8,128)(2,1)} fusion(bf16[512,1536]{1,0:T(8,128)(2,1)} %copy-done.2, bf16[1536,768]{1,0:T(8,128)(2,1)} %param.9), kind=kOutput, calls=%fused_computation.22 | convolution fusion | flops 1208745984 | bytes 4718592 | tf_op jit(solution)/shard_map/dot_general | solution.py:62
  39.3 2.3 %copy.24 = bf16[512,768]{0,1:T(8,128)(2,1)} copy(bf16[512,768]{1,0:T(8,128)(2,1)} %multiply_convert_fusion) | data formatting | bytes 1572864 | tf_op jit(solution)/shard_map/convert_element_type | solution.py:63
  41.6 59.5 %all-gather.3.cloned.1.call-done = bf16[16,128,768]{2,1,0:T(8,128)(2,1)} async-done(((bf16[2,128,768]{2,1,0:T(8,128)(2,1)}), bf16[16,128,768]{2,1,0:T(8,128)(2,1)}) %all-gather.3.cloned.1.call-update) | async-done | bytes 3145744 | tf_op jit(solution)/shard_map/all_gather | solution.py:15
  101.0 2.4 %reduce_sum.31 = bf16[2,128,768]{2,1,0:T(8,128)(2,1)S(1)} reduce(bf16[8,2,128,768]{3,2,1,0:T(8,128)(2,1)} %bitcast.65, bf16[]{:T(256)} %constant.15.clone.1), dimensions={0}, to_apply=%region_1.2 | reduce | flops 1376256 | bytes 3538946 | tf_op jit(solution)/shard_map/reduce_sum | solution.py:15
  103.5 0.0 collective-permute-done.1
  103.5 0.0 collective-permute-done
  103.5 3.0 %maximum_maximum_fusion = bf16[2,1664,768]{2,1,0:T(8,128)(2,1)S(1)} fusion(bf16[1,512,768]{2,1,0:T(8,128)(2,1)S(1)} %fusion.15, bf16[1,512,768]{2,1,0:T(8,128)(2,1)} %fusion.14, bf16[2,512,768]{2,1,0:T(8,128)(2,1)} %collective-permute-done.1, bf16[2,512,768]{2,1,0:T(8,128)(2,1)} %collective-permute-done, bf16[2,128,768]{2,1,0:T(8,128)(2,1)S(1)} %reduce_sum.31), kind=kLoop, calls=%fused_computation.8 | loop fusion | flops 25559040 | bytes 10223616 | tf_op jit(solution)/shard_map/concatenate | solution.py:75
  106.5 2.6 %fusion.30 = (bf16[1,1664,768]{2,1,0:T(8,128)(2,1)}, bf16[1,1664,768]{2,1,0:T(8,128)(2,1)}) fusion(bf16[2,1664,768]{2,1,0:T(8,128)(2,1)S(1)} %maximum_maximum_fusion), kind=kLoop, calls=%fused_computation.49 | loop fusion | bytes 10223616 | tf_op jit(solution)/shard_map/slice | solution.py:79
  109.1 4.5 %copy.21 = bf16[1,1664,768]{1,2,0:T(8,128)(2,1)} copy(bf16[1,1664,768]{2,1,0:T(8,128)(2,1)} %get-tuple-element.6) | data formatting | bytes 5111808 | tf_op jit(solution)/shard_map/slice | solution.py:80
  113.6 0.0 copy-start.3
  113.6 4.7 %copy.25 = bf16[1,1664,768]{1,2,0:T(8,128)(2,1)} copy(bf16[1,1664,768]{2,1,0:T(8,128)(2,1)} %get-tuple-element.5) | data formatting | bytes 5111808 | tf_op jit(solution)/shard_map/slice | solution.py:79
  118.2 0.0 copy-done.3
  118.2 13.3 %fusion.31 = (f32[6,512]{1,0:T(8,128)S(1)}, bf16[6,512,1664]{2,1,0:T(8,128)(2,1)}) fusion(pred[512,1664]{1,0:T(8,128)(4,1)S(1)} %copy-done.3, bf16[512,6,128]{0,2,1:T(8,128)(2,1)} %bitcast.69, bf16[1664,6,128]{0,2,1:T(8,128)(2,1)} %bitcast.67), kind=kOutput, calls=%fused_computation.50 | convolution fusion | flops 1334183552 | bytes 14430208 | tf_op jit(solution)/shard_map/sub | solution.py:92
  131.5 8.1 %fusion.11 = bf16[512,6,128]{0,2,1:T(8,128)(2,1)S(1)} fusion(bf16[1664,6,128]{0,2,1:T(8,128)(2,1)} %bitcast.66, bf16[6,512,1664]{2,1,0:T(8,128)(2,1)} %get-tuple-element.10, f32[512,6]{0,1:T(8,128)S(1)} %bitcast.71), kind=kOutput, calls=%fused_computation.20 | convolution fusion | flops 1309409280 | bytes 13578240 | tf_op jit(solution)/shard_map/hqk,khd->qhd/dot_general | solution.py:95
  139.6 0.0 copy-done
  139.6 3.1 %fusion.32 = f32[512,1536]{1,0:T(8,128)} fusion(bf16[512,768]{0,1:T(8,128)(2,1)S(1)} %bitcast.68, bf16[768,1536]{1,0:T(8,128)(2,1)S(1)} %copy-done), kind=kOutput, calls=%fused_computation.52 | convolution fusion | flops 1207959552 | bytes 6291456 | tf_op jit(solution)/shard_map/dot_general | solution.py:103
  142.7 0.0 reduce-scatter.2.cloned.1.call-update
  142.7 3.5 %convert_element_type.27 = f32[512,1536]{1,0:T(8,128)} convert(bf16[512,1536]{1,0:T(8,128)(2,1)} %param.8) | non-fusion elementwise | flops 786432 | bytes 4718592 | tf_op jit(solution)/shard_map/convert_element_type | solution.py:42
  146.2 68.2 %reduce-scatter.2.cloned.1.call-done = f32[512,768]{1,0:T(8,128)} async-done(((f32[512,1536]{1,0:T(8,128)}), f32[512,768]{1,0:T(8,128)}) %reduce-scatter.2.cloned.1.call-update) | async-done | bytes 1572880 | tf_op jit(solution)/shard_map/reduce_scatter | solution.py:104
  214.4 2.9 %add_convert_fusion = bf16[512,768]{1,0:T(8,128)(2,1)} fusion(f32[512,768]{1,0:T(8,128)} %reduce-scatter.2.cloned.1.call-done, f32[512,1536]{1,0:T(8,128)} %convert_element_type.27, s32[]{:T(128)S(6)} %select_n.18), kind=kLoop, calls=%fused_computation.21 | loop fusion | flops 786432 | bytes 3932164 | tf_op jit(solution)/shard_map/convert_element_type | solution.py:106
  (4 shorter events, 0.0 us)
Async XLA Ops:
  6.5 133.1 %copy-start = (bf16[768,1536]{1,0:T(8,128)(2,1)S(1)}, bf16[768,1536]{1,0:T(8,128)(2,1)}, u32[]{:S(2)}) copy-start(bf16[768,1536]{1,0:T(8,128)(2,1)} %param.12) | copy-start | bytes 7077892
  6.5 94.5 %all-gather.3.cloned.1.call-start = ((), (), s32[]{:S(2)}) async-start(), calls=%async_computation.2 | async-start | bytes 3538944 | tf_op jit(solution)/shard_map/all_gather | solution.py:15
  6.5 3.2 %copy-start.1 = (bf16[512,1536]{1,0:T(8,128)(2,1)S(1)}, bf16[512,1536]{1,0:T(8,128)(2,1)}, u32[]{:S(2)}) copy-start(bf16[512,1536]{1,0:T(8,128)(2,1)} %param.8) | copy-start | bytes 4718596
  6.5 3.8 %copy-start.5 = (bf16[1536,768]{1,0:T(8,128)(2,1)S(1)}, bf16[1536,768]{1,0:T(8,128)(2,1)}, u32[]{:S(2)}) copy-start(bf16[1536,768]{1,0:T(8,128)(2,1)} %param.11) | copy-start | bytes 7077892
  10.3 1.4 copy-start.2
  10.3 2.2 copy-start.6
  14.8 13.8 %copy-start.4 = (s32[1,4,13]{2,1,0:T(4,128)S(1)}, s32[1,4,13]{2,1,0:T(4,128)}, u32[]{:S(2)}) copy-start(s32[1,4,13]{2,1,0:T(4,128)} %param.13) | copy-start | bytes 628
  16.6 197.8 %reduce-scatter.2.cloned.1.call-start = ((), (), s32[]{:S(2)}) async-start(), calls=%async_computation.1 | async-start | bytes 4718592 | tf_op jit(solution)/shard_map/reduce_scatter | solution.py:104
  19.1 84.4 %collective-permute-start.1 = (bf16[2,512,768]{2,1,0:T(8,128)(2,1)}, bf16[2,512,768]{2,1,0:T(8,128)(2,1)}, u32[]{:S(2)}, u32[]{:S(2)}) collective-permute-start(bf16[2,512,768]{2,1,0:T(8,128)(2,1)} %pad_maximum_fusion), channel_id=1, source_target_pairs={{0,4},{4,8},{8,12},{12,16},{16,20},{20,24},{24,28},{1,5},{5,9},{9,... | collective-permute-start | bytes 4718600 | tf_op jit(solution)/shard_map/ppermute | solution.py:21
  25.1 78.4 %collective-permute-start = (bf16[2,512,768]{2,1,0:T(8,128)(2,1)}, bf16[2,512,768]{2,1,0:T(8,128)(2,1)}, u32[]{:S(2)}, u32[]{:S(2)}) collective-permute-start(bf16[2,512,768]{2,1,0:T(8,128)(2,1)} %pad_maximum_fusion), channel_id=1, source_target_pairs={{0,8},{4,12},{8,16},{12,20},{16,24},{20,28},{1,9},{5,13},{9,17},{1... | collective-permute-start | bytes 4718600 | tf_op jit(solution)/shard_map/ppermute | solution.py:21
  113.6 4.7 %copy-start.3 = (pred[512,1664]{1,0:T(8,128)(4,1)S(1)}, pred[512,1664]{1,0:T(8,128)(4,1)}, u32[]{:S(2)}) copy-start(pred[512,1664]{1,0:T(8,128)(4,1)} %copy.23) | copy-start | bytes 2555908
Sparse Core Ops, SparseCore 0:
  16.7 84.2 all-gather.2
  142.8 71.5 reduce-scatter.1
